TPU v7x, 32 devices: a whole 2x2x4 slice. The times are simulated.
32 devices in a mesh: grid: 4 (over x, core), comp: 8 (over z, y).
Axes of the slice: x: 2, y: 2, z: 4, core: 2. Of those that a mesh axis runs over, the one named last changes fastest.
Arguments:
- spectra: float32 [32, 32, 36, 2048], P('comp', None, None, 'grid'), may hold values from 0.1 to 2
- u_wind: float32 [32, 2048], P(None, 'grid'), may hold values from 2 to 20
- wind_dir: float32 [32, 2048], P(None, 'grid'), may hold values from -3.140625 to 3.140625
- sea_mask: int32 [32, 2048], P(None, 'grid'), may hold values from 0 to 1, as said below
Outputs:
- spectra_next: float32 [32, 32, 36, 2048], P('comp', None, None, 'grid')
Inputs may be any that keep to these rules, and one draw needn't show every extreme that they name: sea_mask is 1 at sea and 0 on land; land lies in rectangular blocks of rows and columns.
All inputs are finite; a program needn't handle non-finite values.
Results may differ from a plain program's by a relative error of at most 0.00016.
Values sent between devices are 32-bit elements; how exact they have to be, the bound alone decides.
No kernel may reach another device: no remote copies, remote signals or barrier semaphores. Data moves between devices by JAX's collectives and lax.ppermute only.
A program may use at most 192 MiB of HBM per device.

v0:
```python
import math
import jax
import jax.numpy as jnp
from jax import lax
from jax.sharding import PartitionSpec as P

GRAVITY = 9.81
FREQ_LOW = 0.04
FREQ_RATIO = 1.1
LAMBDA = 0.25
SOURCE_STEP = 120.0
ADVECT_STEP = 220.0
WIND_FACTOR = 0.0003125
TRANSFER_FACTOR = 0.1
EARTH_RADIUS = 6371000.0
BAND_CENTRE = 30.0
CELL_DEGREES = 0.05
CELL_RADIANS = CELL_DEGREES * math.pi / 180.0
ANGLE_NEAR = 11.48
ANGLE_FAR = 33.56
FREQ_UPPER_SHIFT = math.log(1.0 + LAMBDA) / math.log(FREQ_RATIO)
FREQ_LOWER_SHIFT = math.log(1.0 - LAMBDA) / math.log(FREQ_RATIO)
WEIGHT_UPPER = 1.0 / (1.0 + LAMBDA) ** 4
WEIGHT_LOWER = 1.0 / (1.0 - LAMBDA) ** 4
WEIGHT_CROSS = 2.0 / (1.0 - LAMBDA * LAMBDA) ** 4
HIGHEST = lax.Precision.HIGHEST


def padded_2(block, sides, width):
    for axis, dim in sides:
        count = lax.axis_size(axis)
        forward = [(i, i + 1) for i in range(count - 1)]
        backward = [(target, source) for source, target in forward]
        low = lax.ppermute(
            lax.slice_in_dim(block, block.shape[dim] - width, None, axis=dim), axis, forward
        )
        high = lax.ppermute(lax.slice_in_dim(block, 0, width, axis=dim), axis, backward)
        block = jnp.concatenate([low, block, high], axis=dim)
    return block


def hat_matrix(bin_count, bin_shift, periodic):
    target = jnp.arange(bin_count, dtype=jnp.float32)[:, None] + bin_shift
    source = jnp.arange(bin_count, dtype=jnp.float32)[None, :]
    offset_gap = target - source
    if periodic:
        offset_gap = jnp.mod(offset_gap + bin_count / 2.0, float(bin_count)) - bin_count / 2.0
    return jnp.maximum(0.0, 1.0 - jnp.abs(offset_gap))


def nonlinear(point_block):
    freq_count = point_block.shape[0]
    dir_count = point_block.shape[2]
    freq_upper = hat_matrix(freq_count, FREQ_UPPER_SHIFT, False)
    freq_lower = hat_matrix(freq_count, FREQ_LOWER_SHIFT, False)
    spread_upper = jnp.einsum("km,mrjq->krjq", freq_upper, point_block, precision=HIGHEST)
    spread_lower = jnp.einsum("km,mrjq->krjq", freq_lower, point_block, precision=HIGHEST)
    near_bins = ANGLE_NEAR * dir_count / 360.0
    far_bins = ANGLE_FAR * dir_count / 360.0
    squared = point_block * point_block
    centre_total = jnp.zeros_like(point_block)
    back_upper = jnp.zeros_like(point_block)
    back_lower = jnp.zeros_like(point_block)
    for shifts in ((near_bins, -far_bins), (-near_bins, far_bins)):
        dir_upper = hat_matrix(dir_count, shifts[0], True)
        dir_lower = hat_matrix(dir_count, shifts[1], True)
        plus_value = jnp.einsum("jn,krnq->krjq", dir_upper, spread_upper, precision=HIGHEST)
        minus_value = jnp.einsum("jn,krnq->krjq", dir_lower, spread_lower, precision=HIGHEST)
        interaction = TRANSFER_FACTOR * (
            squared * (plus_value * WEIGHT_UPPER + minus_value * WEIGHT_LOWER)
            - WEIGHT_CROSS * point_block * plus_value * minus_value
        )
        centre_total = centre_total - 2.0 * interaction
        back_upper = back_upper + jnp.einsum(
            "jn,krjq->krnq", dir_upper, interaction, precision=HIGHEST
        )
        back_lower = back_lower + jnp.einsum(
            "jn,krjq->krnq", dir_lower, interaction, precision=HIGHEST
        )
    centre_total = centre_total + jnp.einsum(
        "km,krjq->mrjq", freq_upper, back_upper, precision=HIGHEST
    )
    return centre_total + jnp.einsum("km,krjq->mrjq", freq_lower, back_lower, precision=HIGHEST)


def frequency(freq_index):
    return (FREQ_LOW * jnp.power(FREQ_RATIO, freq_index.astype(jnp.float32))).reshape(-1, 1, 1, 1)


def wind_growth(freq, angles, wind_speed, heading):
    radian_freq = 2.0 * math.pi * freq
    celerity = GRAVITY / radian_freq
    alignment = jnp.cos(angles) * jnp.cos(heading) + jnp.sin(angles) * jnp.sin(heading)
    return (
        WIND_FACTOR
        * SOURCE_STEP
        * radian_freq
        * jnp.maximum(0.0, wind_speed / celerity * alignment - 1.0)
    )


def courant_x(freq, angles, row_index, total_rows):
    group_speed = GRAVITY / (4.0 * math.pi * freq)
    latitude = BAND_CENTRE + (row_index.astype(jnp.float32) - (total_rows - 1) / 2.0) * CELL_DEGREES
    row_cos = jnp.cos(latitude * (math.pi / 180.0)).reshape(1, -1, 1, 1)
    return group_speed * jnp.cos(angles) * ADVECT_STEP / (EARTH_RADIUS * row_cos * CELL_RADIANS)


def courant_y(freq, angles):
    group_speed = GRAVITY / (4.0 * math.pi * freq)
    return group_speed * jnp.sin(angles) * ADVECT_STEP / (EARTH_RADIUS * CELL_RADIANS)


def latitude_cos(total_rows):
    cell_lat = (
        BAND_CENTRE
        + (jnp.arange(total_rows, dtype=jnp.float32) - (total_rows - 1) / 2.0) * CELL_DEGREES
    )
    face_lat = (
        BAND_CENTRE
        + (jnp.arange(total_rows + 1, dtype=jnp.float32) - total_rows / 2.0) * CELL_DEGREES
    )
    cell_cos = jnp.cos(cell_lat * (math.pi / 180.0)).reshape(1, -1, 1, 1)
    face_cos = jnp.cos(face_lat * (math.pi / 180.0)).reshape(1, -1, 1, 1)
    return (face_cos, 1.0 / cell_cos)


def advect(padded, courant, face_weight, cell_weight, along_axis):
    cells = padded.shape[along_axis] - 4

    def piece_at(offset_cells, length_cells):
        return lax.slice_in_dim(padded, offset_cells, offset_cells + length_cells, axis=along_axis)

    left_cell = piece_at(1, cells + 1)
    right_cell = piece_at(2, cells + 1)
    far_left = piece_at(0, cells + 1)
    far_right = piece_at(3, cells + 1)
    curvature = jnp.where(
        courant >= 0.0,
        right_cell - 2.0 * left_cell + far_left,
        far_right - 2.0 * right_cell + left_cell,
    )
    face_value = (
        0.5 * (left_cell + right_cell)
        - 0.5 * courant * (right_cell - left_cell)
        - (1.0 - courant * courant) / 6.0 * curvature
    )
    flux_face = courant * face_value * face_weight
    difference = lax.slice_in_dim(flux_face, 1, cells + 1, axis=along_axis) - lax.slice_in_dim(
        flux_face, 0, cells, axis=along_axis
    )
    return piece_at(2, cells) - difference * cell_weight


def shards(spectra, u_wind, wind_dir, sea_mask):
    freq_local, band_rows, dir_count, lon_cells = spectra.shape
    comp_count = lax.axis_size("comp")
    block_rows = band_rows // comp_count
    comp_index = lax.axis_index("comp")
    mask_field = sea_mask.astype(jnp.float32)[None, :, None, :]
    masked = spectra * mask_field
    angles = (jnp.arange(dir_count, dtype=jnp.float32) * (2.0 * math.pi / dir_count)).reshape(
        1, 1, -1, 1
    )
    own_freq = frequency(comp_index * freq_local + jnp.arange(freq_local, dtype=jnp.int32))
    flattened = masked.reshape(freq_local, comp_count, block_rows, dir_count, lon_cells)
    point_block = lax.all_to_all(flattened, "comp", split_axis=1, concat_axis=0, tiled=True)[:, 0]
    all_freq = frequency(jnp.arange(freq_local * comp_count, dtype=jnp.int32))
    start_row = comp_index * block_rows
    speed_rows = lax.dynamic_slice_in_dim(u_wind, start_row, block_rows, 0)[None, :, None, :]
    heading_rows = lax.dynamic_slice_in_dim(wind_dir, start_row, block_rows, 0)[None, :, None, :]
    growth = wind_growth(all_freq, angles, speed_rows, heading_rows)
    post = point_block * (1.0 + growth) + nonlinear(point_block)
    padded = padded_2(post, (("grid", 3),), 2)
    mask_rows = lax.dynamic_slice_in_dim(sea_mask, start_row, block_rows, 0).astype(jnp.float32)[
        None, :, None, :
    ]
    row_index = start_row + jnp.arange(block_rows, dtype=jnp.int32)
    crossing = courant_x(all_freq, angles, row_index, band_rows)
    swept_points = advect(padded, crossing, 1.0, 1.0, 3) * mask_rows
    swept_x = lax.all_to_all(swept_points[:, None], "comp", split_axis=0, concat_axis=1, tiled=True)
    swept_x = swept_x.reshape(freq_local, band_rows, dir_count, lon_cells)
    padded_rows = jnp.pad(swept_x, ((0, 0), (2, 2), (0, 0), (0, 0)))
    face_cos, cell_inverse = latitude_cos(band_rows)
    return advect(padded_rows, courant_y(own_freq, angles), face_cos, cell_inverse, 1) * mask_field


def solution(mesh):
    return jax.shard_map(
        shards,
        mesh=mesh,
        in_specs=(P("comp", None, None, "grid"), P(None, "grid"), P(None, "grid"), P(None, "grid")),
        out_specs=P("comp", None, None, "grid"),
        check_vma=False,
    )
```

profile of v0, /device:TPU:1, one launch (start us, length us, event | category | flops | bytes accessed | tf_op | source)
XLA Modules:
  0.0 902.1 jit_solution(3873852487964017667)
XLA Ops:
  1.5 9.7 %broadcast_multiply_fusion.2 = f32[4,32,36,512]{3,1,2,0:T(8,128)} fusion(f32[4,32,36,512]{3,1,2,0:T(8,128)} %param.4, f32[32,512]{1,0:T(8,128)S(1)} %convert_element_type.37), kind=kLoop, calls=%fused_computation.70 | loop fusion | flops 2359296 | bytes 18939904 | tf_op jit(solution)/shard_map/mul | solution.py:161
  11.2 13.4 %copy.35 = f32[4,32,36,512]{3,0,2,1:T(4,128)} copy(f32[4,32,36,512]{3,1,2,0:T(8,128)} %broadcast_multiply_fusion.2) | data formatting | bytes 18874368 | tf_op jit(solution)/shard_map/mul | solution.py:161
  24.6 6.6 all-to-all-start
  34.0 201.9 %all-to-all-done = f32[4,8,4,36,512]{4,0,3,2,1:T(4,128)} async-done(((f32[4,8,4,36,512]{4,0,3,2,1:T(4,128)}), f32[4,8,4,36,512]{4,0,3,2,1:T(4,128)}, u32[]{:S(2)}, u32[]{:S(2)}) %all-to-all-start) | async-done | bytes 9437216 | tf_op jit(solution)/shard_map/all_to_all | solution.py:167
  235.9 10.3 %copy.36 = f32[8,4,1,4,36,512]{5,1,0,4,3,2:T(4,128)} copy(f32[8,4,1,4,36,512]{5,1,4,3,0,2:T(4,128)} %bitcast.2) | data formatting | bytes 18874368 | tf_op jit(solution)/shard_map/all_to_all | solution.py:167
  246.3 12.0 %squeeze.3 = f32[32,4,36,512]{3,0,2,1:T(8,128)} reshape(f32[8,4,1,4,36,512]{5,1,0,4,3,2:T(4,128)} %copy.36) | data formatting | bytes 18874368 | tf_op jit(solution)/shard_map/squeeze | solution.py:167
  258.2 13.3 %fusion.97 = f32[32,4,36,512]{3,0,2,1:T(8,128)S(1)} fusion(f32[32,4,36,512]{3,0,2,1:T(8,128)} %squeeze.3, f32[32]{0:T(128)S(1)} %get-tuple-element.19), kind=kOutput, calls=%fused_computation.122 | convolution fusion | flops 905973760 | bytes 18874496 | tf_op jit(solution)/shard_map/km,mrjq->krjq/dot_general | solution.py:56
  271.5 21.1 %fusion.27 = f32[32,4,512,36]{2,3,1,0:T(8,128)} fusion(f32[32,4,36,512]{3,0,2,1:T(8,128)S(1)} %fusion.97, f32[36]{0:T(128)S(1)} %iota_add_fusion.2), kind=kOutput, calls=%fused_computation.37 | convolution fusion | flops 1019231424 | bytes 18874512 | tf_op jit(solution)/shard_map/jn,krnq->krjq/dot_general | solution.py:67
  292.7 21.4 %fusion.29 = f32[32,4,512,36]{2,3,1,0:T(8,128)} fusion(f32[32,4,36,512]{3,0,2,1:T(8,128)S(1)} %fusion.97, f32[36]{0:T(128)S(1)} %iota_add_fusion.5), kind=kOutput, calls=%fused_computation.39 | convolution fusion | flops 1019231424 | bytes 18874512 | tf_op jit(solution)/shard_map/jn,krnq->krjq/dot_general | solution.py:67
  314.2 9.3 %fusion.94 = f32[32,4,36,512]{3,0,2,1:T(8,128)S(1)} fusion(f32[32,4,36,512]{3,0,2,1:T(8,128)S(1)} %bitcast.116, f32[32]{0:T(128)S(1)} %iota_add_fusion.4), kind=kOutput, calls=%fused_computation.119 | convolution fusion | flops 905973760 | bytes 18874496 | tf_op jit(solution)/shard_map/km,mrjq->krjq/dot_general | solution.py:57
  323.5 21.0 %fusion.23 = f32[32,4,512,36]{2,3,1,0:T(8,128)} fusion(f32[32,4,36,512]{3,0,2,1:T(8,128)S(1)} %fusion.94, f32[36]{0:T(128)S(1)} %iota_add_fusion.1), kind=kOutput, calls=%fused_computation.33 | convolution fusion | flops 1019231424 | bytes 18874512 | tf_op jit(solution)/shard_map/jn,krnq->krjq/dot_general | solution.py:68
  344.5 21.1 %fusion.25 = f32[32,4,512,36]{2,3,1,0:T(8,128)} fusion(f32[32,4,36,512]{3,0,2,1:T(8,128)S(1)} %fusion.94, f32[36]{0:T(128)S(1)} %iota_add_fusion.3), kind=kOutput, calls=%fused_computation.35 | convolution fusion | flops 1019231424 | bytes 18874512 | tf_op jit(solution)/shard_map/jn,krnq->krjq/dot_general | solution.py:68
  365.6 39.8 %broadcast_multiply_fusion.1 = (f32[32,4,36,512]{3,0,2,1:T(8,128)}, f32[32,4,36,512]{3,0,2,1:T(8,128)S(1)}) fusion(f32[32,4,36,512]{3,0,2,1:T(8,128)S(1)} %bitcast.116, f32[32,4,512,36]{2,3,1,0:T(8,128)} %fusion.25, f32[32,4,512,36]{2,3,1,0:T(8,128)} %fusion.29, f32[32,4,512,36]{2,3,1,0:T(8,128)} %fusion.23, f32[32,4,512,36]{2,3,1,0:T(8,128)} %fusion.27), kind=kLoop, calls=%fused_computation.69 | loop fusion | flops 42467328 | bytes 66060288 | tf_op jit(solution)/shard_map/mul | solution.py:69
  405.4 21.7 %fusion.15 = f32[32,4,512,36]{2,3,1,0:T(8,128)} fusion(f32[32,4,36,512]{3,0,2,1:T(8,128)S(1)} %get-tuple-element.8, f32[36]{0:T(128)S(1)} %iota_add_fusion.1), kind=kOutput, calls=%fused_computation.25 | convolution fusion | flops 1019231424 | bytes 18874512 | tf_op jit(solution)/shard_map/jn,krjq->krnq/dot_general | solution.py:77
  427.1 21.2 %fusion.17 = f32[32,4,512,36]{2,3,1,0:T(8,128)} fusion(f32[32,4,36,512]{3,0,2,1:T(8,128)S(1)} %get-tuple-element.8, f32[36]{0:T(128)S(1)} %iota_add_fusion.2), kind=kOutput, calls=%fused_computation.27 | convolution fusion | flops 1019231424 | bytes 18874512 | tf_op jit(solution)/shard_map/jn,krjq->krnq/dot_general | solution.py:74
  448.4 22.5 %add_bitcast_fusion = f32[32,4,36,512]{3,2,1,0:T(8,128)} fusion(f32[32,4,512,36]{2,3,1,0:T(8,128)} %fusion.15, f32[32,4,36,512]{3,0,2,1:T(8,128)S(1)} %bitcast.120, f32[36]{0:T(128)S(1)} %iota_add_fusion.3), kind=kOutput, calls=%fused_computation.23 | convolution fusion | flops 1021590720 | bytes 28311696 | tf_op jit(solution)/shard_map/jn,krjq->krnq/dot_general | solution.py:77
  470.9 19.4 %fusion.43 = f32[32,4,36,512]{3,0,2,1:T(8,128)} fusion(f32[32,4,36,512]{3,2,1,0:T(8,128)} %add_bitcast_fusion, f32[32]{0:T(128)S(1)} %iota_add_fusion.4), kind=kOutput, calls=%fused_computation.63 | convolution fusion | flops 905973760 | bytes 18874496 | tf_op jit(solution)/shard_map/km,krjq->mrjq/dot_general | solution.py:83
  490.4 23.0 %add_bitcast_fusion.1 = f32[32,4,36,512]{3,2,1,0:T(8,128)} fusion(f32[32,4,512,36]{2,3,1,0:T(8,128)S(1)} %bitcast.122, f32[32,4,36,512]{3,0,2,1:T(8,128)S(1)} %bitcast.120, f32[36]{0:T(128)S(1)} %iota_add_fusion.5), kind=kOutput, calls=%fused_computation.24 | convolution fusion | flops 1021590720 | bytes 28311696 | tf_op jit(solution)/shard_map/jn,krjq->krnq/dot_general | solution.py:74
  513.4 63.4 %add_add_fusion = f32[32,4,36,512]{3,0,2,1:T(8,128)} fusion(f32[32,4,36,512]{3,0,2,1:T(8,128)} %fusion.43, f32[32,4,36,512]{3,0,2,1:T(8,128)} %squeeze.3, f32[4,36,512]{2,1,0:T(8,128)S(1)} %multiply_add_fusion, f32[32,4,512]{2,0,1:T(8,128)S(1)} %broadcast_divide_fusion, f32[32]{0:T(128)S(1)} %get-tuple-element.20, ...), kind=kOutput, calls=%fused_computation.67 | convolution fusion | flops 974393344 | bytes 76054784 | tf_op jit(solution)/shard_map/km,krjq->mrjq/dot_general | solution.py:80
  576.9 4.7 fusion.211
  584.5 4.8 collective-permute-start
  594.0 3.0 copy.58
  598.0 4.3 copy.60
  602.3 22.3 %fusion.13 = f32[32,4,36,513]{3,0,2,1:T(8,128)S(1)} fusion(f32[32,4,36,2]{3,0,2,1:T(8,128)} %copy.60, f32[32,4,36,512]{3,0,2,1:T(8,128)} %add_add_fusion, f32[32,4,36,2]{3,0,2,1:T(8,128)S(1)} %copy.58, f32[32,4,36]{0,2,1:T(8,128)} %get-tuple-element.13, f32[32,4,36]{0,2,1:T(8,128)} %get-tuple-element.12, f32[32,4,36]{0,2,1:T(8,128)S(1)} %copy-done.5, ...), kind=kLoop, calls=%fused_computation.18 | loop fusion | flops 44914176 | bytes 19026432 | tf_op jit(solution)/shard_map/mul | solution.py:148
  624.7 5.4 fusion.36
  630.1 13.4 %copy.61 = f32[32,1,4,36,512]{4,2,3,1,0:T(4,128)} copy(f32[32,1,4,36,512]{4,0,3,2,1:T(8,128)} %fusion.36) | data formatting | bytes 18874368 | tf_op jit(solution)/shard_map/broadcast_in_dim | solution.py:181
  643.5 5.4 all-to-all-start.1
  649.2 203.8 %all-to-all-done.1 = f32[32,1,4,36,512]{4,2,3,1,0:T(4,128)} async-done(((f32[32,1,4,36,512]{4,2,3,1,0:T(4,128)}), f32[32,1,4,36,512]{4,2,3,1,0:T(4,128)}, u32[]{:S(2)}, u32[]{:S(2)}) %all-to-all-start.1) | async-done | bytes 9437216 | tf_op jit(solution)/shard_map/all_to_all | solution.py:181
  853.0 10.3 %copy.62 = f32[4,8,1,4,36,512]{5,3,1,4,0,2:T(4,128)} copy(f32[4,8,1,4,36,512]{5,3,4,0,1,2:T(4,128)} %bitcast.29) | data formatting | bytes 18874368 | tf_op jit(solution)/shard_map/all_to_all | solution.py:181
  863.3 11.9 %reshape.297 = f32[4,32,36,512]{3,1,2,0:T(8,128)} reshape(f32[4,8,1,4,36,512]{5,3,1,4,0,2:T(4,128)} %copy.62) | data formatting | bytes 18874368 | tf_op jit(solution)/shard_map/reshape | solution.py:182
  875.3 20.4 %fusion.5 = f32[4,33,36,512]{3,1,2,0:T(8,128)S(1)} fusion(f32[4,32,36,512]{3,1,2,0:T(8,128)} %reshape.297, f32[33]{0:T(128)S(1)} %multiply_cosine_fusion, f32[4,36]{1,0:T(4,128)S(1)} %get-tuple-element.16, f32[4,36]{1,0:T(4,128)S(1)} %get-tuple-element.15, f32[4,36]{1,0:T(4,128)S(1)} %get-tuple-element.14, pred[4,36]{1,0:T(4,128)(4,1)S(1)} %fusion.159), kind=kLoop, calls=%fused_computation.9 | loop fusion | flops 38928384 | bytes 19171284 | tf_op jit(solution)/shard_map/mul | solution.py:148
  895.7 5.9 fusion.33
  (75 shorter events, 13.2 us)
Async XLA Ops:
  0.0 31.4 %copy-start = (f32[32,512]{1,0:T(8,128)S(1)}, f32[32,512]{1,0:T(8,128)}, u32[]{:S(2)}) copy-start(f32[32,512]{1,0:T(8,128)} %param.5) | copy-start | bytes 196612
  0.9 0.6 copy-start.3
  24.6 211.4 %all-to-all-start = ((f32[4,8,4,36,512]{4,0,3,2,1:T(4,128)}), f32[4,8,4,36,512]{4,0,3,2,1:T(4,128)}, u32[]{:S(2)}, u32[]{:S(2)}) async-start(f32[4,8,4,36,512]{4,0,3,2,1:T(4,128)} %bitcast.123), calls=%async_computation | async-start | bytes 18874368 | tf_op jit(solution)/shard_map/all_to_all | solution.py:167
  31.4 2.5 copy-start.7
  271.5 42.6 %slice-start = ((s8[9437184]{0:T(1024)(128)(4,1)}), s8[4194304]{0:T(1024)(128)(4,1)S(1)}, s32[]{:S(2)}) async-start(s8[9437184]{0:T(1024)(128)(4,1)} %bitcast.115), calls=%async_computation.2 | async-start | bytes 8388608
  271.5 42.6 %slice-start.1 = ((s8[9437184]{0:T(1024)(128)(4,1)}), s8[4194304]{0:T(1024)(128)(4,1)S(1)}, s32[]{:S(2)}) async-start(s8[9437184]{0:T(1024)(128)(4,1)} %bitcast.115), calls=%async_computation.3 | async-start | bytes 8388608
  292.7 21.5 %slice-start.2 = ((s8[9437184]{0:T(1024)(128)(4,1)}), s8[1048576]{0:T(1024)(128)(4,1)S(1)}, s32[]{:S(2)}) async-start(s8[9437184]{0:T(1024)(128)(4,1)} %bitcast.115), calls=%async_computation.4 | async-start | bytes 2097152
  405.4 42.9 %slice-start.6 = ((s8[9437184]{0:T(1024)(128)(4,1)}), s8[4194304]{0:T(1024)(128)(4,1)S(1)}, s32[]{:S(2)}) async-start(s8[9437184]{0:T(1024)(128)(4,1)} %bitcast.119), calls=%async_computation.8 | async-start | bytes 8388608
  405.4 42.9 %slice-start.7 = ((s8[9437184]{0:T(1024)(128)(4,1)}), s8[4194304]{0:T(1024)(128)(4,1)S(1)}, s32[]{:S(2)}) async-start(s8[9437184]{0:T(1024)(128)(4,1)} %bitcast.119), calls=%async_computation.9 | async-start | bytes 8388608
  427.1 21.2 %slice-start.8 = ((s8[9437184]{0:T(1024)(128)(4,1)}), s8[1048576]{0:T(1024)(128)(4,1)S(1)}, s32[]{:S(2)}) async-start(s8[9437184]{0:T(1024)(128)(4,1)} %bitcast.119), calls=%async_computation.10 | async-start | bytes 2097152
  448.4 42.0 %slice-start.9 = ((s8[10485760]{0:T(1024)(128)(4,1)}), s8[4194304]{0:T(1024)(128)(4,1)S(1)}, s32[]{:S(2)}) async-start(s8[10485760]{0:T(1024)(128)(4,1)} %bitcast.121), calls=%async_computation.11 | async-start | bytes 8388608
  448.4 42.0 %slice-start.10 = ((s8[10485760]{0:T(1024)(128)(4,1)}), s8[4194304]{0:T(1024)(128)(4,1)S(1)}, s32[]{:S(2)}) async-start(s8[10485760]{0:T(1024)(128)(4,1)} %bitcast.121), calls=%async_computation.12 | async-start | bytes 8388608
  470.9 19.5 %slice-start.11 = ((s8[10485760]{0:T(1024)(128)(4,1)}), s8[2097152]{0:T(1024)(128)(4,1)S(1)}, s32[]{:S(2)}) async-start(s8[10485760]{0:T(1024)(128)(4,1)} %bitcast.121), calls=%async_computation.13 | async-start | bytes 4194304
  576.8 25.5 %copy-start.5 = (f32[32,4,36]{0,2,1:T(8,128)S(1)}, f32[32,4,36]{0,2,1:T(8,128)}, u32[]{:S(2)}) copy-start(f32[32,4,36]{0,2,1:T(8,128)} %get-tuple-element.11) | copy-start | bytes 55300
  576.8 25.5 %copy-start.6 = (pred[32,4,36]{0,2,1:T(8,128)(4,1)S(1)}, pred[32,4,36]{0,2,1:T(8,128)(4,1)}, u32[]{:S(2)}) copy-start(pred[32,4,36]{0,2,1:T(8,128)(4,1)} %broadcast_compare_fusion) | copy-start | bytes 13828
  584.5 9.5 %collective-permute-start = (f32[32,4,36,2]{2,0,3,1:T(8,128)S(1)}, f32[32,4,36,2]{2,0,3,1:T(8,128)}, u32[]{:S(2)}, u32[]{:S(2)}) collective-permute-start(f32[32,4,36,2]{2,0,3,1:T(8,128)S(1)} %copy.57), channel_id=1, source_target_pairs={{0,8},{8,16},{16,24},{1,9},{9,17},{17,25},{2,10},{10,18},{18,26},{... | collective-permute-start | bytes 110600 | tf_op jit(solution)/shard_map/ppermute | solution.py:34
  591.4 6.6 collective-permute-start.1
  598.0 26.7 %slice-start.3 = ((s8[9437184]{0:T(1024)(128)(4,1)}), s8[1048576]{0:T(1024)(128)(4,1)S(1)}, s32[]{:S(2)}) async-start(s8[9437184]{0:T(1024)(128)(4,1)} %bitcast.117), calls=%async_computation.5 | async-start | bytes 2097152
  602.3 22.4 %slice-start.4 = ((s8[9437184]{0:T(1024)(128)(4,1)}), s8[4194304]{0:T(1024)(128)(4,1)S(1)}, s32[]{:S(2)}) async-start(s8[9437184]{0:T(1024)(128)(4,1)} %bitcast.117), calls=%async_computation.6 | async-start | bytes 8388608
  602.3 22.4 %slice-start.5 = ((s8[9437184]{0:T(1024)(128)(4,1)}), s8[4194304]{0:T(1024)(128)(4,1)S(1)}, s32[]{:S(2)}) async-start(s8[9437184]{0:T(1024)(128)(4,1)} %bitcast.117), calls=%async_computation.7 | async-start | bytes 8388608
  643.5 5.6 copy-start.8
  643.5 209.5 %all-to-all-start.1 = ((f32[32,1,4,36,512]{4,2,3,1,0:T(4,128)}), f32[32,1,4,36,512]{4,2,3,1,0:T(4,128)}, u32[]{:S(2)}, u32[]{:S(2)}) async-start(f32[32,1,4,36,512]{4,2,3,1,0:T(4,128)} %copy.61), calls=%async_computation.1 | async-start | bytes 18874368 | tf_op jit(solution)/shard_map/all_to_all | solution.py:181
  875.3 20.4 %copy-start.2 = (f32[4,32,36,512]{3,1,2,0:T(8,128)S(1)}, f32[4,32,36,512]{3,1,2,0:T(8,128)}, u32[]{:S(2)}) copy-start(f32[4,32,36,512]{3,1,2,0:T(8,128)} %reshape.297) | copy-start | bytes 28311556
  875.3 20.5 %copy-start.4 = (f32[32,512]{1,0:T(8,128)S(1)}, f32[32,512]{1,0:T(8,128)}, u32[]{:S(2)}) copy-start(f32[32,512]{1,0:T(8,128)} %copy-done.3) | copy-start | bytes 196612
  895.7 5.9 copy-start.1
where the time goes:
time: 909 us; the launch traced here: 902 us
  waiting for transfers between devices  407 us (45%)
  matrix products  279 us (31%)
  other arithmetic  107 us (12%)
  local copies, waits for them, and re-layouts  90 us (10%)
  starting transfers between devices  18.7 us (2%)
    all_to_all x1, waiting for transfers between devices, shards(): lax.all_to_all(swept_points[:, None], 'comp', split_axis=0, concat_axis=1...  204 us
    all_to_all x1, waiting for transfers between devices, shards(): lax.all_to_all(flattened, 'comp', split_axis=1, concat_axis=0, tiled=True)  202 us
    dot_general x1, matrix products, nonlinear(): jnp.einsum('km,krjq->mrjq', freq_upper, back_upper, precision=HIGHEST)  63.4 us
    dot_general x2, matrix products, nonlinear(): jnp.einsum('jn,krjq->krnq', dir_lower, interaction, precision=HIGHEST)  44.2 us
    dot_general x2, matrix products, nonlinear(): jnp.einsum('jn,krjq->krnq', dir_upper, interaction, precision=HIGHEST)  44.2 us
    mul x2, other arithmetic, advect(): flux_face = courant * face_value * face_weight  42.8 us
    dot_general x2, matrix products, nonlinear(): jnp.einsum('jn,krnq->krjq', dir_upper, spread_upper, precision=HIGHEST)  42.6 us
    dot_general x2, matrix products, nonlinear(): jnp.einsum('jn,krnq->krjq', dir_lower, spread_lower, precision=HIGHEST)  42.1 us
  transfers between devices with their start and end apart: 4, of which 3 were waited for; matrix products, arithmetic and copies ran while one was open for 1% of the time, Pallas kernels for 0%

commit v1 on v0

--- a/solution.py
+++ b/solution.py
@@ -24,6 +24,25 @@
 WEIGHT_LOWER = 1.0 / (1.0 - LAMBDA) ** 4
 WEIGHT_CROSS = 2.0 / (1.0 - LAMBDA * LAMBDA) ** 4
 HIGHEST = lax.Precision.HIGHEST
+
+
+def axis_part_close(axis_key, field):
+    frame_out = jax.lax.axis_size(axis_key)
+    t_next, o_now = (frame_out, jax.lax.axis_index(axis_key))
+    outer = list(field.shape)
+    a_next = field.shape[1] // t_next
+    outer[1] = a_next
+    piece_out = outer[0]
+    outer[0] = piece_out * t_next
+    t1 = jnp.zeros(outer, field.dtype)
+    for hop_no in range(t_next):
+        g_now = lax.dynamic_slice_in_dim(field, (o_now ^ hop_no) * a_next, a_next, axis=1)
+        if hop_no:
+            g_now = jax.lax.ppermute(
+                g_now, axis_key, perm=[(no, no ^ hop_no) for no in range(t_next)]
+            )
+        t1 = lax.dynamic_update_slice_in_dim(t1, g_now, (o_now ^ hop_no) * piece_out, axis=0)
+    return t1
 
 
 def padded_2(block, sides, width):
@@ -164,7 +183,7 @@
     )
     own_freq = frequency(comp_index * freq_local + jnp.arange(freq_local, dtype=jnp.int32))
     flattened = masked.reshape(freq_local, comp_count, block_rows, dir_count, lon_cells)
-    point_block = lax.all_to_all(flattened, "comp", split_axis=1, concat_axis=0, tiled=True)[:, 0]
+    point_block = axis_part_close("comp", flattened)[:, 0]
     all_freq = frequency(jnp.arange(freq_local * comp_count, dtype=jnp.int32))
     start_row = comp_index * block_rows
     speed_rows = lax.dynamic_slice_in_dim(u_wind, start_row, block_rows, 0)[None, :, None, :]

time: 909 us -> 850 us (0.935)
  waiting for transfers between devices: 407 us -> 325 us
  starting transfers between devices: 18.7 us -> 67.9 us
  matrix products: 279 us -> 241 us
  local copies, waits for them, and re-layouts: 90 us -> 108 us
    all_to_all x1 -> x0, waiting for transfers between devices: 202 us -> none  [shards(): lax.all_to_all(flattened, 'comp', split_axis=1, concat_axis=0, tiled=True)]
    ppermute x0 -> x7, waiting for transfers between devices: none -> 119 us  [axis_part_close(): jax.lax.ppermute(g_now, axis_key, perm=[(no, no ^ hop_no) for no in range...]
    dot_general x1, matrix products: 63.4 us -> 19.6 us  [nonlinear(): jnp.einsum('km,krjq->mrjq', freq_upper, back_upper, precision=HIGHEST)]
    all_to_all x1, starting transfers between devices: 5.44 us -> 48.5 us  [shards(): lax.all_to_all(swept_points[:, None], 'comp', split_axis=0, concat_axis=1...]
    mul x1, other arithmetic: 39.8 us -> 0.55 us  [wind_growth(): WIND_FACTOR * SOURCE_STEP * radian_freq]
    dot_general x2, matrix products: 42.6 us -> 64.9 us  [nonlinear(): jnp.einsum('jn,krnq->krjq', dir_upper, spread_upper, precision=HIGHEST)]
    add x0 -> x1, other arithmetic: none -> 22 us  [shards(): post = point_block * (1.0 + growth) + nonlinear(point_block)]
    dynamic_slice x0 -> x8, local copies, waits for them, and re-layouts: none -> 18.1 us  [axis_part_close(): lax.dynamic_slice_in_dim(field, (o_now ^ hop_no) * a_next, a_next, axis=1)]
  transfers between devices with their start and end apart: 4 -> 10, of which waited for: 3 -> 5; matrix products, arithmetic and copies ran while one was open for 1% -> 5% of each run, Pallas kernels for 0% -> 0%
where the time goes in v1:
time: 850 us; the launch traced here: 841 us
  waiting for transfers between devices  325 us (38%)
  matrix products  241 us (28%)
  local copies, waits for them, and re-layouts  108 us (13%)
  other arithmetic  98.2 us (12%)
  starting transfers between devices  67.9 us (8%)
    all_to_all x1, waiting for transfers between devices, shards(): lax.all_to_all(swept_points[:, None], 'comp', split_axis=0, concat_axis=1...  204 us
    ppermute x7, waiting for transfers between devices, axis_part_close(): jax.lax.ppermute(g_now, axis_key, perm=[(no, no ^ hop_no) for no in range...  119 us
    dot_general x2, matrix products, nonlinear(): jnp.einsum('jn,krnq->krjq', dir_upper, spread_upper, precision=HIGHEST)  64.9 us
    all_to_all x1, starting transfers between devices, shards(): lax.all_to_all(swept_points[:, None], 'comp', split_axis=0, concat_axis=1...  48.5 us
    mul x2, other arithmetic, advect(): flux_face = courant * face_value * face_weight  46.9 us
    dot_general x2, matrix products, nonlinear(): jnp.einsum('jn,krnq->krjq', dir_lower, spread_lower, precision=HIGHEST)  41.8 us
    dot_general x2, matrix products, nonlinear(): jnp.einsum('jn,krjq->krnq', dir_upper, interaction, precision=HIGHEST)  32.8 us
    dot_general x2, matrix products, nonlinear(): jnp.einsum('jn,krjq->krnq', dir_lower, interaction, precision=HIGHEST)  26.4 us
  transfers between devices with their start and end apart: 10, of which 5 were waited for; matrix products, arithmetic and copies ran while one was open for 5% of the time, Pallas kernels for 0%

profile of v1, /device:TPU:1, one launch (start us, length us, event | category | flops | bytes accessed | tf_op | source)
XLA Modules:
  0.0 840.6 jit_solution(7124358905017122853)
XLA Ops:
  1.5 9.7 %broadcast_multiply_fusion = f32[4,32,36,512]{3,1,2,0:T(8,128)} fusion(f32[4,32,36,512]{3,1,2,0:T(8,128)} %param.4, f32[32,512]{1,0:T(8,128)S(1)} %convert_element_type.37), kind=kLoop, calls=%fused_computation.78 | loop fusion | flops 2359296 | bytes 18939904 | tf_op jit(solution)/shard_map/mul | solution.py:180
  11.2 13.4 %copy.36 = f32[4,32,36,512]{3,0,2,1:T(4,128)} copy(f32[4,32,36,512]{3,1,2,0:T(8,128)} %broadcast_multiply_fusion) | data formatting | bytes 18874368 | tf_op jit(solution)/shard_map/mul | solution.py:180
  24.6 6.4 constant_dynamic-slice_fusion.1
  51.1 5.3 squeeze.19
  63.0 3.4 collective-permute-start.5
  69.1 41.0 %collective-permute-done.1 = f32[4,1,4,36,512]{4,2,3,1,0:T(4,128)} collective-permute-done((f32[4,1,4,36,512]{4,2,3,1,0:T(4,128)}, f32[4,1,4,36,512]{4,2,3,1,0:T(4,128)}, u32[]{:S(2)}, u32[]{:S(2)}) %collective-permute-start.1) | collective-permute-done | bytes 1179680 | tf_op jit(solution)/shard_map/ppermute | solution.py:41
  112.9 21.5 %collective-permute-done.2 = f32[4,1,4,36,512]{4,2,3,1,0:T(4,128)} collective-permute-done((f32[4,1,4,36,512]{4,2,3,1,0:T(4,128)}, f32[4,1,4,36,512]{4,2,3,1,0:T(4,128)}, u32[]{:S(2)}, u32[]{:S(2)}) %collective-permute-start.2) | collective-permute-done | bytes 1179680 | tf_op jit(solution)/shard_map/ppermute | solution.py:41
  139.8 56.6 %collective-permute-done.4 = f32[4,1,4,36,512]{4,2,3,1,0:T(4,128)} collective-permute-done((f32[4,1,4,36,512]{4,2,3,1,0:T(4,128)}, f32[4,1,4,36,512]{4,2,3,1,0:T(4,128)}, u32[]{:S(2)}, u32[]{:S(2)}) %collective-permute-start.4) | collective-permute-done | bytes 1179680 | tf_op jit(solution)/shard_map/ppermute | solution.py:41
  202.1 17.7 %fusion.48 = f32[32,4,36,512]{3,0,2,1:T(8,128)S(1)} fusion(f32[32,4,36,512]{3,2,1,0:T(8,128)} %bitcast_dynamic-update-slice_fusion, f32[32]{0:T(128)S(1)} %iota_add_fusion.4), kind=kOutput, calls=%fused_computation.70 | convolution fusion | flops 905973760 | bytes 18874496 | tf_op jit(solution)/shard_map/km,mrjq->krjq/dot_general | solution.py:76
  219.8 18.1 %fusion.50 = f32[32,4,36,512]{3,0,2,1:T(8,128)} fusion(f32[32,4,36,512]{3,2,1,0:T(8,128)} %bitcast_dynamic-update-slice_fusion, f32[32]{0:T(128)S(1)} %copy-done.10), kind=kOutput, calls=%fused_computation.72 | convolution fusion | flops 905973760 | bytes 18874496 | tf_op jit(solution)/shard_map/km,mrjq->krjq/dot_general | solution.py:75
  237.9 21.0 %fusion.25 = f32[32,4,512,36]{2,3,1,0:T(8,128)} fusion(f32[32,4,36,512]{3,0,2,1:T(8,128)S(1)} %fusion.48, f32[36]{0:T(128)S(1)} %copy-done.17), kind=kOutput, calls=%fused_computation.46 | convolution fusion | flops 1019231424 | bytes 18874512 | tf_op jit(solution)/shard_map/jn,krnq->krjq/dot_general | solution.py:87
  258.9 30.7 %fusion.20 = f32[32,4,36,512]{3,2,1,0:T(8,128)} fusion(f32[32,4,512,36]{2,3,1,0:T(8,128)} %fusion.25, f32[32,4,36,512]{3,2,1,0:T(8,128)} %bitcast_dynamic-update-slice_fusion, f32[32,4,36,512]{3,0,2,1:T(8,128)} %fusion.50, f32[36]{0:T(128)} %iota_add_fusion.2), kind=kOutput, calls=%fused_computation.31 | convolution fusion | flops 1040465088 | bytes 37748880 | tf_op jit(solution)/shard_map/jn,krnq->krjq/dot_general | solution.py:86
  289.6 15.4 %fusion.35 = f32[32,4,512,36]{2,3,1,0:T(8,128)} fusion(f32[32,4,36,512]{3,2,1,0:T(8,128)} %fusion.20, f32[36]{0:T(128)} %iota_add_fusion.2), kind=kOutput, calls=%fused_computation.56 | convolution fusion | flops 1021590720 | bytes 18874512 | tf_op jit(solution)/shard_map/jn,krjq->krnq/dot_general | solution.py:93
  305.0 12.4 %fusion.33 = f32[32,4,512,36]{2,3,1,0:T(8,128)} fusion(f32[32,4,36,512]{3,2,1,0:T(8,128)S(1)} %copy-done.2, f32[36]{0:T(128)S(1)} %copy-done.18), kind=kOutput, calls=%fused_computation.54 | convolution fusion | flops 1021590720 | bytes 18874512 | tf_op jit(solution)/shard_map/jn,krjq->krnq/dot_general | solution.py:96
  317.5 20.8 %fusion.27 = f32[32,4,512,36]{2,3,1,0:T(8,128)} fusion(f32[32,4,36,512]{3,0,2,1:T(8,128)S(1)} %fusion.48, f32[36]{0:T(128)S(1)} %copy-done.14), kind=kOutput, calls=%fused_computation.48 | convolution fusion | flops 1019231424 | bytes 18874512 | tf_op jit(solution)/shard_map/jn,krnq->krjq/dot_general | solution.py:87
  338.3 34.2 %fusion.23 = f32[32,4,36,512]{3,2,1,0:T(8,128)} fusion(f32[32,4,512,36]{2,3,1,0:T(8,128)} %fusion.27, f32[32,4,36,512]{3,2,1,0:T(8,128)} %bitcast_dynamic-update-slice_fusion, f32[32,4,36,512]{3,0,2,1:T(8,128)} %fusion.50, f32[36]{0:T(128)} %iota_add_fusion.5), kind=kOutput, calls=%fused_computation.38 | convolution fusion | flops 1040465088 | bytes 37748880 | tf_op jit(solution)/shard_map/jn,krnq->krjq/dot_general | solution.py:86
  372.6 17.4 %add_bitcast_fusion.1 = f32[32,4,36,512]{3,2,1,0:T(8,128)} fusion(f32[32,4,512,36]{2,3,1,0:T(8,128)} %fusion.35, f32[32,4,36,512]{3,2,1,0:T(8,128)} %fusion.23, f32[36]{0:T(128)S(1)} %copy-done.16), kind=kOutput, calls=%fused_computation.45 | convolution fusion | flops 1023950016 | bytes 28311696 | tf_op jit(solution)/shard_map/jn,krjq->krnq/dot_general | solution.py:93
  389.9 19.6 %fusion.46 = f32[32,4,36,512]{3,0,2,1:T(8,128)} fusion(f32[32,4,36,512]{3,2,1,0:T(8,128)} %add_bitcast_fusion.1, f32[32]{0:T(128)S(1)} %copy-done.11), kind=kOutput, calls=%fused_computation.68 | convolution fusion | flops 905973760 | bytes 18874496 | tf_op jit(solution)/shard_map/km,krjq->mrjq/dot_general | solution.py:99
  409.6 13.9 %add_bitcast_fusion = f32[32,4,36,512]{3,2,1,0:T(8,128)} fusion(f32[32,4,512,36]{2,3,1,0:T(8,128)} %fusion.33, f32[32,4,36,512]{3,2,1,0:T(8,128)S(1)} %bitcast.111, f32[36]{0:T(128)S(1)} %copy-done.15), kind=kOutput, calls=%fused_computation.44 | convolution fusion | flops 1023950016 | bytes 28311696 | tf_op jit(solution)/shard_map/jn,krjq->krnq/dot_general | solution.py:96
  423.5 19.6 %fusion.44 = f32[32,4,36,512]{3,0,2,1:T(8,128)} fusion(f32[32,4,36,512]{3,2,1,0:T(8,128)} %add_bitcast_fusion, f32[32]{0:T(128)S(1)} %iota_add_fusion.4), kind=kOutput, calls=%fused_computation.66 | convolution fusion | flops 905973760 | bytes 18874496 | tf_op jit(solution)/shard_map/km,krjq->mrjq/dot_general | solution.py:102
  443.2 22.0 %fusion.24 = f32[32,4,36,512]{3,2,1,0:T(8,128)} fusion(f32[32,4,36,512]{3,0,2,1:T(8,128)} %fusion.44, f32[32,4,36,512]{3,0,2,1:T(8,128)} %fusion.46, f32[32,4,36,512]{3,2,1,0:T(8,128)S(1)} %bitcast.109, f32[32,4,36,512]{3,2,1,0:T(8,128)S(1)} %bitcast.111, f32[32,4,36,512]{3,2,1,0:T(8,128)} %bitcast_dynamic-update-slice_fusion, ...), kind=kLoop, calls=%fused_computation.42 | loop fusion | flops 30670848 | bytes 57180288 | tf_op jit(solution)/shard_map/add | solution.py:192
  465.2 4.9 fusion.224
  472.8 7.2 collective-permute-start.7
  489.9 26.6 %fusion.5 = f32[32,4,36,513]{3,2,1,0:T(8,128)S(1)} fusion(f32[32,4,36,2]{3,2,1,0:T(8,128)} %copy.71, f32[32,4,36,512]{3,2,1,0:T(8,128)} %fusion.24, f32[32,4,36,2]{3,2,1,0:T(8,128)} %copy.69, f32[32,4,36]{2,1,0:T(4,128)S(1)} %copy-done.8, f32[32,4,36]{2,1,0:T(4,128)S(1)} %get-tuple-element.18, f32[32,4,36]{2,1,0:T(4,128)S(1)} %get-tuple-element.17, ...), kind=kLoop, calls=%fused_computation.10 | loop fusion | flops 44914176 | bytes 19026432 | tf_op jit(solution)/shard_map/mul | solution.py:167
  516.6 6.1 fusion.17
  522.7 15.7 %copy.72 = f32[32,1,4,36,512]{4,2,3,1,0:T(4,128)} copy(f32[32,1,4,36,512]{4,3,2,0,1:T(8,128)} %fusion.17) | data formatting | bytes 18874368 | tf_op jit(solution)/shard_map/broadcast_in_dim | solution.py:200
  538.4 48.5 %all-to-all-start = ((f32[32,1,4,36,512]{4,2,3,1,0:T(4,128)}), f32[32,1,4,36,512]{4,2,3,1,0:T(4,128)}, u32[]{:S(2)}, u32[]{:S(2)}) async-start(f32[32,1,4,36,512]{4,2,3,1,0:T(4,128)} %copy.72), calls=%async_computation | async-start | bytes 18874368 | tf_op jit(solution)/shard_map/all_to_all | solution.py:200
  587.2 204.5 %all-to-all-done = f32[32,1,4,36,512]{4,2,3,1,0:T(4,128)} async-done(((f32[32,1,4,36,512]{4,2,3,1,0:T(4,128)}), f32[32,1,4,36,512]{4,2,3,1,0:T(4,128)}, u32[]{:S(2)}, u32[]{:S(2)}) %all-to-all-start) | async-done | bytes 9437216 | tf_op jit(solution)/shard_map/all_to_all | solution.py:200
  791.7 10.3 %copy.73 = f32[4,8,1,4,36,512]{5,3,1,4,0,2:T(4,128)} copy(f32[4,8,1,4,36,512]{5,3,4,0,1,2:T(4,128)} %bitcast.35) | data formatting | bytes 18874368 | tf_op jit(solution)/shard_map/all_to_all | solution.py:200
  802.0 11.9 %reshape.312 = f32[4,32,36,512]{3,1,2,0:T(8,128)} reshape(f32[4,8,1,4,36,512]{5,3,1,4,0,2:T(4,128)} %copy.73) | data formatting | bytes 18874368 | tf_op jit(solution)/shard_map/reshape | solution.py:201
  813.9 20.3 %fusion.12 = f32[4,33,36,512]{3,1,2,0:T(8,128)S(1)} fusion(f32[4,32,36,512]{3,1,2,0:T(8,128)} %reshape.312, f32[33]{0:T(128)S(1)} %multiply_cosine_fusion, f32[4,36]{1,0:T(4,128)S(1)} %get-tuple-element.22, f32[4,36]{1,0:T(4,128)S(1)} %get-tuple-element.21, f32[4,36]{1,0:T(4,128)S(1)} %get-tuple-element.20, pred[4,36]{1,0:T(4,128)(4,1)S(1)} %fusion.168), kind=kLoop, calls=%fused_computation.20 | loop fusion | flops 38928384 | bytes 19171284 | tf_op jit(solution)/shard_map/mul | solution.py:167
  834.3 5.9 fusion.43
  (118 shorter events, 57.6 us)
Async XLA Ops:
  0.0 50.2 %copy-start = (f32[32,512]{1,0:T(8,128)S(1)}, f32[32,512]{1,0:T(8,128)}, u32[]{:S(2)}) copy-start(f32[32,512]{1,0:T(8,128)} %param.5) | copy-start | bytes 196612
  32.8 30.2 %collective-permute-start = (f32[4,1,4,36,512]{4,2,3,1,0:T(4,128)}, f32[4,1,4,36,512]{4,2,3,1,0:T(4,128)}, u32[]{:S(2)}, u32[]{:S(2)}) collective-permute-start(f32[4,1,4,36,512]{4,2,3,1,0:T(4,128)} %copy.38), channel_id=1, source_target_pairs={{0,1},{1,0},{2,3},{3,2},{4,5},{5,4},{6,7},{7,6},{8,9},{9,8},{10,11... | collective-permute-start | bytes 3538952 | tf_op jit(solution)/shard_map/ppermute | solution.py:41
  36.6 73.5 %collective-permute-start.1 = (f32[4,1,4,36,512]{4,2,3,1,0:T(4,128)}, f32[4,1,4,36,512]{4,2,3,1,0:T(4,128)}, u32[]{:S(2)}, u32[]{:S(2)}) collective-permute-start(f32[4,1,4,36,512]{4,2,3,1,0:T(4,128)} %copy.40), channel_id=1, source_target_pairs={{0,2},{1,3},{2,0},{3,1},{4,6},{5,7},{6,4},{7,5},{8,10},{9,11},{10,... | collective-permute-start | bytes 3538952 | tf_op jit(solution)/shard_map/ppermute | solution.py:41
  39.9 94.5 %collective-permute-start.2 = (f32[4,1,4,36,512]{4,2,3,1,0:T(4,128)}, f32[4,1,4,36,512]{4,2,3,1,0:T(4,128)}, u32[]{:S(2)}, u32[]{:S(2)}) collective-permute-start(f32[4,1,4,36,512]{4,2,3,1,0:T(4,128)} %copy.42), channel_id=1, source_target_pairs={{0,3},{1,2},{2,1},{3,0},{4,7},{5,6},{6,5},{7,4},{8,11},{9,10},{10,... | collective-permute-start | bytes 3538952 | tf_op jit(solution)/shard_map/ppermute | solution.py:41
  41.7 95.4 %collective-permute-start.3 = (f32[4,1,4,36,512]{4,2,3,1,0:T(4,128)}, f32[4,1,4,36,512]{4,2,3,1,0:T(4,128)}, u32[]{:S(2)}, u32[]{:S(2)}) collective-permute-start(f32[4,1,4,36,512]{4,2,3,1,0:T(4,128)} %copy.44), channel_id=1, source_target_pairs={{0,4},{1,5},{2,6},{3,7},{4,0},{5,1},{6,2},{7,3},{8,12},{9,13},{10,... | collective-permute-start | bytes 3538952 | tf_op jit(solution)/shard_map/ppermute | solution.py:41
  45.9 150.6 %collective-permute-start.4 = (f32[4,1,4,36,512]{4,2,3,1,0:T(4,128)}, f32[4,1,4,36,512]{4,2,3,1,0:T(4,128)}, u32[]{:S(2)}, u32[]{:S(2)}) collective-permute-start(f32[4,1,4,36,512]{4,2,3,1,0:T(4,128)} %copy.46), channel_id=1, source_target_pairs={{0,5},{1,4},{2,7},{3,6},{4,1},{5,0},{6,3},{7,2},{8,13},{9,12},{10,... | collective-permute-start | bytes 3538952 | tf_op jit(solution)/shard_map/ppermute | solution.py:41
  49.2 20.0 %copy-start.12 = (f32[36]{0:T(128)}, f32[36]{0:T(128)S(1)}, u32[]{:S(2)}) copy-start(f32[36]{0:T(128)S(1)} %get-tuple-element.23) | copy-start | bytes 436
  63.0 136.2 %collective-permute-start.5 = (f32[4,1,4,36,512]{4,2,3,1,0:T(4,128)}, f32[4,1,4,36,512]{4,2,3,1,0:T(4,128)S(1)}, u32[]{:S(2)}, u32[]{:S(2)}) collective-permute-start(f32[4,1,4,36,512]{4,2,3,1,0:T(4,128)} %copy.48), channel_id=1, source_target_pairs={{0,6},{1,7},{2,4},{3,5},{4,2},{5,3},{6,0},{7,1},{8,14},{9,15},{10,... | collective-permute-start | bytes 3538952 | tf_op jit(solution)/shard_map/ppermute | solution.py:41
  110.1 90.5 %collective-permute-start.6 = (f32[4,1,4,36,512]{4,2,3,1,0:T(4,128)S(1)}, f32[4,1,4,36,512]{4,2,3,1,0:T(4,128)S(1)}, u32[]{:S(2)}, u32[]{:S(2)}) collective-permute-start(f32[4,1,4,36,512]{4,2,3,1,0:T(4,128)S(1)} %copy.50), channel_id=1, source_target_pairs={{0,7},{1,6},{2,5},{3,4},{4,3},{5,2},{6,1},{7,0},{8,15},{9,14},{10,... | collective-permute-start | bytes 3538952 | tf_op jit(solution)/shard_map/ppermute | solution.py:41
  200.6 19.2 %copy-start.10 = (f32[32]{0:T(128)S(1)}, f32[32]{0:T(128)}, u32[]{:S(2)}) copy-start(f32[32]{0:T(128)} %iota_add_fusion.6) | copy-start | bytes 388
  338.3 34.2 %copy-start.16 = (f32[36]{0:T(128)S(1)}, f32[36]{0:T(128)}, u32[]{:S(2)}) copy-start(f32[36]{0:T(128)} %iota_add_fusion.5) | copy-start | bytes 436
  372.6 37.0 %slice-start.3 = ((s8[10485760]{0:T(1024)(128)(4,1)}), s8[4194304]{0:T(1024)(128)(4,1)S(1)}, s32[]{:S(2)}) async-start(s8[10485760]{0:T(1024)(128)(4,1)} %bitcast.110), calls=%async_computation.4 | async-start | bytes 8388608
  372.6 37.0 %slice-start.4 = ((s8[10485760]{0:T(1024)(128)(4,1)}), s8[4194304]{0:T(1024)(128)(4,1)S(1)}, s32[]{:S(2)}) async-start(s8[10485760]{0:T(1024)(128)(4,1)} %bitcast.110), calls=%async_computation.5 | async-start | bytes 8388608
  389.9 19.6 %slice-start.5 = ((s8[10485760]{0:T(1024)(128)(4,1)}), s8[2097152]{0:T(1024)(128)(4,1)S(1)}, s32[]{:S(2)}) async-start(s8[10485760]{0:T(1024)(128)(4,1)} %bitcast.110), calls=%async_computation.6 | async-start | bytes 4194304
  389.9 19.6 %copy-start.15 = (f32[36]{0:T(128)S(1)}, f32[36]{0:T(128)}, u32[]{:S(2)}) copy-start(f32[36]{0:T(128)} %iota_add_fusion.3) | copy-start | bytes 436
  409.5 33.6 %slice-start = ((s8[10485760]{0:T(1024)(128)(4,1)}), s8[4194304]{0:T(1024)(128)(4,1)S(1)}, s32[]{:S(2)}) async-start(s8[10485760]{0:T(1024)(128)(4,1)} %bitcast.108), calls=%async_computation.1 | async-start | bytes 8388608
  409.5 33.6 %slice-start.1 = ((s8[10485760]{0:T(1024)(128)(4,1)}), s8[2097152]{0:T(1024)(128)(4,1)S(1)}, s32[]{:S(2)}) async-start(s8[10485760]{0:T(1024)(128)(4,1)} %bitcast.108), calls=%async_computation.2 | async-start | bytes 4194304
  423.5 19.6 %slice-start.2 = ((s8[10485760]{0:T(1024)(128)(4,1)}), s8[4194304]{0:T(1024)(128)(4,1)S(1)}, s32[]{:S(2)}) async-start(s8[10485760]{0:T(1024)(128)(4,1)} %bitcast.108), calls=%async_computation.3 | async-start | bytes 8388608
  423.5 19.6 %copy-start.5 = (f32[32,4,512]{2,1,0:T(4,128)S(1)}, f32[32,4,512]{2,1,0:T(4,128)}, u32[]{:S(2)}) copy-start(f32[32,4,512]{2,1,0:T(4,128)} %broadcast_divide_fusion) | copy-start | bytes 786436
  423.5 19.6 %copy-start.19 = (f32[32]{0:T(128)S(1)}, f32[32]{0:T(128)}, u32[]{:S(2)}) copy-start(f32[32]{0:T(128)} %fusion.171) | copy-start | bytes 388
  465.2 24.7 %copy-start.8 = (f32[32,4,36]{2,1,0:T(4,128)S(1)}, f32[32,4,36]{2,1,0:T(4,128)}, u32[]{:S(2)}) copy-start(f32[32,4,36]{2,1,0:T(4,128)} %get-tuple-element.19) | copy-start | bytes 55300
  465.2 24.7 %copy-start.9 = (pred[32,4,36]{2,1,0:T(4,128)(4,1)S(1)}, pred[32,4,36]{2,1,0:T(4,128)(4,1)}, u32[]{:S(2)}) copy-start(pred[32,4,36]{2,1,0:T(4,128)(4,1)} %broadcast_compare_fusion) | copy-start | bytes 13828
  472.8 10.9 %collective-permute-start.7 = (f32[32,4,36,2]{2,0,3,1:T(8,128)S(1)}, f32[32,4,36,2]{2,0,3,1:T(8,128)S(1)}, u32[]{:S(2)}, u32[]{:S(2)}) collective-permute-start(f32[32,4,36,2]{2,0,3,1:T(8,128)S(1)} %copy.68), channel_id=1, source_target_pairs={{0,8},{8,16},{16,24},{1,9},{9,17},{17,25},{2,10},{10,18},{18,26},{... | collective-permute-start | bytes 110600 | tf_op jit(solution)/shard_map/ppermute | solution.py:53
  481.1 6.3 collective-permute-start.8
  487.4 29.2 %slice-start.6 = ((s8[10485760]{0:T(1024)(128)(4,1)}), s8[2097152]{0:T(1024)(128)(4,1)S(1)}, s32[]{:S(2)}) async-start(s8[10485760]{0:T(1024)(128)(4,1)} %bitcast.112), calls=%async_computation.7 | async-start | bytes 4194304
  489.9 26.7 %slice-start.7 = ((s8[10485760]{0:T(1024)(128)(4,1)}), s8[4194304]{0:T(1024)(128)(4,1)S(1)}, s32[]{:S(2)}) async-start(s8[10485760]{0:T(1024)(128)(4,1)} %bitcast.112), calls=%async_computation.8 | async-start | bytes 8388608
  489.9 26.7 %slice-start.8 = ((s8[10485760]{0:T(1024)(128)(4,1)}), s8[4194304]{0:T(1024)(128)(4,1)S(1)}, s32[]{:S(2)}) async-start(s8[10485760]{0:T(1024)(128)(4,1)} %bitcast.112), calls=%async_computation.9 | async-start | bytes 8388608
  538.4 48.7 %copy-start.13 = (f32[36]{0:T(128)S(1)}, f32[36]{0:T(128)}, u32[]{:S(2)}) copy-start(f32[36]{0:T(128)} %copy-done.12) | copy-start | bytes 436
  538.4 253.3 %all-to-all-start = ((f32[32,1,4,36,512]{4,2,3,1,0:T(4,128)}), f32[32,1,4,36,512]{4,2,3,1,0:T(4,128)}, u32[]{:S(2)}, u32[]{:S(2)}) async-start(f32[32,1,4,36,512]{4,2,3,1,0:T(4,128)} %copy.72), calls=%async_computation | async-start | bytes 18874368 | tf_op jit(solution)/shard_map/all_to_all | solution.py:200
  813.9 20.3 %copy-start.3 = (f32[4,32,36,512]{3,1,2,0:T(8,128)S(1)}, f32[4,32,36,512]{3,1,2,0:T(8,128)}, u32[]{:S(2)}) copy-start(f32[4,32,36,512]{3,1,2,0:T(8,128)} %reshape.312) | copy-start | bytes 28311556
  813.9 20.3 %copy-start.7 = (f32[32,512]{1,0:T(8,128)S(1)}, f32[32,512]{1,0:T(8,128)}, u32[]{:S(2)}) copy-start(f32[32,512]{1,0:T(8,128)} %copy-done.6) | copy-start | bytes 196612
  813.9 26.2 %copy-start.1 = (f32[32,512]{1,0:T(8,128)S(1)}, f32[32,512]{1,0:T(8,128)}, u32[]{:S(2)}) copy-start(f32[32,512]{1,0:T(8,128)} %param.5) | copy-start | bytes 196612
  (7 other events, 86.6 us)
